TPU v7x, 128 devices: a whole 4x4x4 slice. The times are simulated.
128 devices in a mesh: req: 16 (over z, y), mp: 8 (over x, core).
Axes of the slice: x: 4, y: 4, z: 4, core: 2. Of those that a mesh axis runs over, the one named last changes fastest.
Arguments:
- q_pre: bfloat16 [8192, 3072], P('req', 'mp'), may hold values from -64 to 64
- k_pre: bfloat16 [8192, 1024], P('req', 'mp'), may hold values from -64 to 64
- v_pre: bfloat16 [8192, 1024], P('req', 'mp'), may hold values from -12 to 12
- q_bias: float32 [3072], P('mp'), may hold values from -3 to 3
- k_bias: float32 [1024], P('mp'), may hold values from -3 to 3
- v_bias: float32 [1024], P('mp'), may hold values from -3 to 3
- segment_ids: int32 [8192], P('req'), may hold values from -1 to 63, as said below
- lengths: int32 [16, 4], replicated, may hold values from 64 to 128, as said below
- page_table: int32 [16, 4], replicated, may hold values from 0 to 63, as said below
- w_out: bfloat16 [3072, 5120], P('mp'), may hold values from -0.109375 to 0.109375
- residual: bfloat16 [8192, 5120], P('req'), may hold values from -4 to 4
- norm_gain: float32 [5120], replicated, may hold values from 0.1 to 1.9
- w_gate: bfloat16 [5120, 6912], P('req', 'mp'), may hold values from -0.078125 to 0.078125
- w_up: bfloat16 [5120, 6912], P('req', 'mp'), may hold values from -0.078125 to 0.078125
Outputs:
- hidden: bfloat16 [8192, 6912], P('req', 'mp')
- kv_cache: bfloat16 [64, 8, 128, 256], P('req', 'mp')
Inputs may be any that keep to these rules, and one draw needn't show every extreme that they name: Requests of block r lie in order from the block's first token, request j taking lengths[r, j] tokens; in every block one request has exactly 128 tokens. `segment_ids`: token t of block r carries r * 4 + j inside request j's run of tokens given by lengths, and -1 after the last request of its block. `page_table`: every page is named once; page p is held by req index p // 4; the requests of one block have pages held by different req indices.
All inputs are finite; a program needn't handle non-finite values.
Results may differ from a plain program's by a relative error of at most 0.019.
Values may be sent and summed in bfloat16 or wider, within the bound.
A program may use at most 128 MiB of HBM per device.

v0:
```python
import math
import jax
import jax.numpy as jnp
from jax import lax
from jax.sharding import PartitionSpec as P

HD = 128
PAGE = 128
REQS = 4
THETA = 1000000.0
EPS = 1e-06


def rotate(values, positions):
    half_dim = values.shape[-1] // 2
    frequencies = THETA ** (-jnp.arange(half_dim, dtype=jnp.float32) * (2.0 / values.shape[-1]))
    angles = positions[:, None] * frequencies[None, :]
    cosine = jnp.cos(angles)[:, None, :]
    sine_part = jnp.sin(angles)[:, None, :]
    first_half = values[..., :half_dim]
    second = values[..., half_dim:]
    return jnp.concatenate(
        [first_half * cosine - second * sine_part, second * cosine + first_half * sine_part],
        axis=-1,
    )


def attend(queries, keys, values, length):
    scale_factor = 1.0 / math.sqrt(queries.shape[-1])
    scores = (
        jnp.einsum("sqhge,skhe->shgqk", queries, keys, preferred_element_type=jnp.float32)
        * scale_factor
    )
    page_len = queries.shape[1]
    query_pos = jnp.arange(page_len)[:, None]
    key_pos = jnp.arange(page_len)[None, :]
    allowed = (key_pos <= query_pos)[None] & (key_pos[None] < length[:, None, None])
    allowed = allowed[:, None, None]
    row_max = jnp.max(jnp.where(allowed, scores, -1e30), axis=-1, keepdims=True)
    weights = jnp.where(allowed, jnp.exp(scores - row_max), 0.0)
    row_sum = jnp.sum(weights, axis=-1, keepdims=True)
    present = (jnp.arange(page_len)[None, :] < length[:, None])[:, None, None, :, None]
    row_probs = jnp.where(present, weights / jnp.where(present, row_sum, 1.0), 0.0).astype(
        jnp.bfloat16
    )
    mixed_rows = jnp.einsum(
        "shgqk,skhe->sqhge", row_probs, values, preferred_element_type=jnp.float32
    )
    return mixed_rows.astype(jnp.bfloat16)


def normalize(resid_rows, summed, gain_row):
    state = resid_rows.astype(jnp.float32) + summed
    scale_row = lax.rsqrt(jnp.mean(state * state, axis=-1, keepdims=True) + EPS)
    return (state * scale_row * gain_row).astype(jnp.bfloat16)


def shards(
    q_pre,
    k_pre,
    v_pre,
    q_bias,
    k_bias,
    v_bias,
    segment_ids,
    lengths,
    page_table,
    w_out,
    residual,
    norm_gain,
    w_gate,
    w_up,
):
    me_req = lax.axis_index("req")
    groups_all = lax.axis_size("req")
    block_rows = q_pre.shape[0]
    kv_heads = k_pre.shape[1] // HD
    q_heads = q_pre.shape[1] // HD
    group_size = q_heads // kv_heads
    own_lens = lax.dynamic_index_in_dim(lengths, me_req, 0, keepdims=False)
    own_pages = lax.dynamic_index_in_dim(page_table, me_req, 0, keepdims=False)
    own_owner = own_pages // REQS
    starts = jnp.cumsum(own_lens) - own_lens
    offsets = jnp.arange(PAGE, dtype=jnp.int32)
    row_index = jnp.clip(starts[:, None] + offsets[None, :], 0, block_rows - 1)
    flat_index = row_index.reshape(-1)
    request_ids = me_req * REQS + jnp.arange(REQS, dtype=jnp.int32)[:, None]
    inside = (offsets[None, :] < own_lens[:, None]) & (
        jnp.take(segment_ids, flat_index).reshape(REQS, PAGE) == request_ids
    )
    keep_mask = inside[:, :, None, None]
    positions = offsets.astype(jnp.float32)

    def prepare(source, bias_row, head_count):
        picked = jnp.take(source, flat_index, axis=0).astype(jnp.float32) + bias_row
        return picked.reshape(REQS, PAGE, head_count, HD)

    query_req = jnp.where(
        keep_mask, rotate(prepare(q_pre, q_bias, q_heads), positions), 0.0
    ).astype(jnp.bfloat16)
    key_req = jnp.where(keep_mask, rotate(prepare(k_pre, k_bias, kv_heads), positions), 0.0).astype(
        jnp.bfloat16
    )
    value_req = jnp.where(keep_mask, prepare(v_pre, v_bias, kv_heads), 0.0).astype(jnp.bfloat16)
    to_owner = (own_owner[None, :] == jnp.arange(groups_all)[:, None]).astype(jnp.bfloat16)
    alive_rows = segment_ids >= 0
    req_idx = jnp.clip(segment_ids - me_req * REQS, 0, REQS - 1)
    req_hit = req_idx[:, None] == jnp.arange(REQS)[None, :]
    row_start = jnp.sum(jnp.where(req_hit, starts[None, :], 0), axis=1)
    row_pos = jnp.clip(jnp.arange(block_rows, dtype=jnp.int32) - row_start, 0, PAGE - 1)
    hits = (
        page_table[None, :, :] == (me_req * REQS + jnp.arange(REQS, dtype=jnp.int32))[:, None, None]
    )
    page_select = jnp.sum(hits.astype(jnp.int32), axis=2).astype(jnp.bfloat16)
    q_send = jnp.einsum(
        "gj,jpc->gpc",
        to_owner,
        query_req.reshape(REQS, PAGE, q_heads * HD),
        preferred_element_type=jnp.float32,
    ).astype(jnp.bfloat16)
    k_send = jnp.einsum(
        "gj,jpc->gpc",
        to_owner,
        key_req.reshape(REQS, PAGE, kv_heads * HD),
        preferred_element_type=jnp.float32,
    ).astype(jnp.bfloat16)
    v_send = jnp.einsum(
        "gj,jpc->gpc",
        to_owner,
        value_req.reshape(REQS, PAGE, kv_heads * HD),
        preferred_element_type=jnp.float32,
    ).astype(jnp.bfloat16)
    q_in, k_in, v_in = (
        lax.all_to_all(q_send, "req", split_axis=0, concat_axis=0, tiled=True),
        lax.all_to_all(k_send, "req", split_axis=0, concat_axis=0, tiled=True),
        lax.all_to_all(v_send, "req", split_axis=0, concat_axis=0, tiled=True),
    )
    in_len = jnp.sum(jnp.where(page_table // REQS == me_req, lengths, 0), axis=1)
    q_groups = q_in.reshape(groups_all, PAGE, kv_heads, group_size, HD)
    k_groups = k_in.reshape(groups_all, PAGE, kv_heads, HD)
    v_groups = v_in.reshape(groups_all, PAGE, kv_heads, HD)
    pages_in = jnp.concatenate([k_groups, v_groups], axis=-1).transpose(0, 2, 1, 3)
    attended = attend(q_groups, k_groups, v_groups, in_len)
    returned = lax.all_to_all(
        attended.reshape(groups_all, PAGE, q_heads * HD),
        "req",
        split_axis=0,
        concat_axis=0,
        tiled=True,
    )
    row_group = jnp.sum(jnp.where(req_hit, own_owner[None, :], 0), axis=1)
    source_rows = jnp.take(
        returned.reshape(groups_all * PAGE, q_heads * HD), row_group * PAGE + row_pos, axis=0
    )
    cache_out = jnp.einsum(
        "ls,shpc->lhpc", page_select, pages_in, preferred_element_type=jnp.float32
    ).astype(jnp.bfloat16)
    attn_rows = jnp.where(alive_rows[:, None], source_rows, jnp.zeros((), jnp.bfloat16))
    summed = lax.psum(
        jnp.dot(attn_rows, w_out, preferred_element_type=jnp.float32).astype(jnp.bfloat16), "mp"
    ).astype(jnp.float32)
    normed = normalize(residual, summed, norm_gain)
    gate_acc = jnp.dot(
        normed,
        lax.all_gather(w_gate, "req", axis=0, tiled=True),
        preferred_element_type=jnp.float32,
    )
    up_acc = jnp.dot(
        normed, lax.all_gather(w_up, "req", axis=0, tiled=True), preferred_element_type=jnp.float32
    )
    hidden = (jax.nn.silu(gate_acc) * up_acc).astype(jnp.bfloat16)
    return (hidden, cache_out)


def solution(mesh):
    in_specs = (
        P("req", "mp"),
        P("req", "mp"),
        P("req", "mp"),
        P("mp"),
        P("mp"),
        P("mp"),
        P("req"),
        P(),
        P(),
        P("mp", None),
        P("req", None),
        P(),
        P("req", "mp"),
        P("req", "mp"),
    )
    out_specs = (P("req", "mp"), P("req", "mp", None, None))
    return jax.shard_map(shards, mesh=mesh, in_specs=in_specs, out_specs=out_specs, check_vma=False)
```

profile of v0, /device:TPU:1, one launch (start us, length us, event | category | flops | bytes accessed | tf_op | source)
XLA Modules:
  0.0 290.8 jit_solution(10564905103255792273)
XLA Ops:
  9.8 3.6 %gather_fusion = s32[512]{0:T(512)S(1)} fusion(s32[512]{0:T(512)} %param.22, s32[1024]{0:T(1024)S(1)} %pad_clamp_fusion.2), kind=kCustom, calls=%fused_computation.2 | custom fusion | bytes 6144 | tf_op jit(solution)/shard_map/jit(_take)/gather | solution.py:89
  13.4 1.9 gather_fusion.1
  18.1 1.5 copy.81
  19.6 8.6 %all-to-all-start.2 = ((bf16[16,128,384]{2,1,0:T(8,128)(2,1)}), bf16[16,128,384]{2,1,0:T(8,128)(2,1)S(1)}, u32[]{:S(2)}, u32[]{:S(2)}) async-start(bf16[16,128,384]{2,1,0:T(8,128)(2,1)} %copy.81), calls=%async_computation.2 | async-start | bytes 3145728 | tf_op jit(solution)/shard_map/all_to_all | solution.py:134
  28.8 1.3 gather_fusion.4
  32.4 1.3 gather_fusion.3
  34.5 16.6 %all-to-all-done.2 = bf16[16,128,384]{2,1,0:T(8,128)(2,1)S(1)} async-done(((bf16[16,128,384]{2,1,0:T(8,128)(2,1)}), bf16[16,128,384]{2,1,0:T(8,128)(2,1)S(1)}, u32[]{:S(2)}, u32[]{:S(2)}) %all-to-all-start.2) | async-done | bytes 1572896 | tf_op jit(solution)/shard_map/all_to_all | solution.py:134
  51.1 4.6 %all-to-all-start.1 = ((bf16[16,128,128]{2,1,0:T(8,128)(2,1)}), bf16[16,128,128]{2,1,0:T(8,128)(2,1)S(1)}, u32[]{:S(2)}, u32[]{:S(2)}) async-start(bf16[16,128,128]{2,1,0:T(8,128)(2,1)} %copy.77), calls=%async_computation.1 | async-start | bytes 1048576 | tf_op jit(solution)/shard_map/all_to_all | solution.py:135
  57.1 1.7 copy.82
  58.7 7.1 %all-to-all-done.1 = bf16[16,128,128]{2,1,0:T(8,128)(2,1)S(1)} async-done(((bf16[16,128,128]{2,1,0:T(8,128)(2,1)}), bf16[16,128,128]{2,1,0:T(8,128)(2,1)S(1)}, u32[]{:S(2)}, u32[]{:S(2)}) %all-to-all-start.1) | async-done | bytes 524320 | tf_op jit(solution)/shard_map/all_to_all | solution.py:135
  65.8 4.2 %all-to-all-start = ((bf16[16,128,128]{2,1,0:T(8,128)(2,1)}), bf16[16,128,128]{2,1,0:T(8,128)(2,1)}, u32[]{:S(2)}, u32[]{:S(2)}) async-start(bf16[16,128,128]{2,1,0:T(8,128)(2,1)} %copy.72), calls=%async_computation | async-start | bytes 1048576 | tf_op jit(solution)/shard_map/all_to_all | solution.py:136
  70.1 2.2 fusion
  73.2 6.2 %all-to-all-done = bf16[16,128,128]{2,1,0:T(8,128)(2,1)} async-done(((bf16[16,128,128]{2,1,0:T(8,128)(2,1)}), bf16[16,128,128]{2,1,0:T(8,128)(2,1)}, u32[]{:S(2)}, u32[]{:S(2)}) %all-to-all-start) | async-done | bytes 524320 | tf_op jit(solution)/shard_map/all_to_all | solution.py:136
  79.4 3.3 %convolution_convert_fusion.1 = bf16[16,128,3,128]{3,1,2,0:T(8,128)(2,1)} fusion(f32[16,128,128,3]{2,1,3,0:T(8,128)S(1)} %get-tuple-element.24, f32[16,3,128]{2,1,0:T(4,128)S(1)} %broadcast_select_fusion, f32[16,3,128]{2,1,0:T(4,128)S(1)} %get-tuple-element.23, pred[16,128,128]{1,2,0:T(8,128)(4,1)S(1)} %broadcast_and_fusion, ...), kind=kOutput, calls=%fused_computation.17 | convolution fusion | flops 206831616 | bytes 5556224 | tf_op jit(solution)/shard_map/shgqk,skhe->sqhge/dot_general | solution.py:46
  82.7 4.0 %all-to-all-start.3 = ((bf16[16,128,384]{1,2,0:T(8,128)(2,1)}), bf16[16,128,384]{1,2,0:T(8,128)(2,1)S(1)}, u32[]{:S(2)}, u32[]{:S(2)}) async-start(bf16[16,128,384]{1,2,0:T(8,128)(2,1)} %bitcast.106), calls=%async_computation.3 | async-start | bytes 3145728 | tf_op jit(solution)/shard_map/all_to_all | solution.py:144
  87.5 18.7 %all-to-all-done.3 = bf16[16,128,384]{1,2,0:T(8,128)(2,1)S(1)} async-done(((bf16[16,128,384]{1,2,0:T(8,128)(2,1)}), bf16[16,128,384]{1,2,0:T(8,128)(2,1)S(1)}, u32[]{:S(2)}, u32[]{:S(2)}) %all-to-all-start.3) | async-done | bytes 1572896 | tf_op jit(solution)/shard_map/all_to_all | solution.py:144
  107.1 1.9 gather_fusion.2
  109.1 6.9 %convolution_convert_fusion = bf16[512,5120]{1,0:T(8,128)(2,1)} fusion(bf16[384,5120]{1,0:T(8,128)(2,1)} %param.25, bf16[512,384]{1,0:T(8,128)(2,1)S(1)} %gather_fusion.2, pred[512]{0:T(512)(128)(4,1)S(1)} %copy-done.12, pred[512]{0:T(512)(128)(4,1)S(1)} %broadcast_compare_fusion), kind=kOutput, calls=%fused_computation.8 | convolution fusion | flops 2016280576 | bytes 9569280 | tf_op jit(solution)/shard_map/dot_general | solution.py:160
  117.6 1.4 copy.109
  120.0 74.5 %all-reduce.2.cloned.1.call-done = bf16[512,5120]{1,0:T(8,128)(2,1)} async-done(((bf16[512,5120]{1,0:T(8,128)(2,1)}), bf16[512,5120]{1,0:T(8,128)(2,1)}) %all-reduce.2.cloned.1.call-update) | async-done | bytes 5242896 | tf_op jit(solution)/shard_map/psum | solution.py:159
  194.5 5.8 %multiply_reduce_fusion = f32[512]{0:T(512)S(1)} fusion(bf16[512,5120]{1,0:T(8,128)(2,1)} %all-reduce.2.cloned.1.call-done, bf16[512,5120]{1,0:T(8,128)(2,1)} %param.26), kind=kLoop, calls=%fused_computation.6 | loop fusion | flops 13106688 | bytes 10487808 | tf_op jit(solution)/shard_map/reduce_sum | solution.py:54
  200.4 12.1 %fusion.51 = f32[512,864]{0,1:T(8,128)S(1)} fusion(bf16[5120,864]{1,0:T(8,128)(2,1)} %all-gather.3.cloned.1.call-done, bf16[512,5120]{1,0:T(8,128)(2,1)} %all-reduce.2.cloned.1.call-done, bf16[512,5120]{1,0:T(8,128)(2,1)} %param.26, f32[5120]{0:T(1024)S(1)} %copy-done.13, f32[512]{0:T(512)S(1)} %add_rsqrt_fusion), kind=kOutput, calls=%fused_computation.124 | convolution fusion | flops 4545576960 | bytes 21125120 | tf_op jit(solution)/shard_map/dot_general | solution.py:163
  212.5 58.1 %all-gather.5.cloned.1.call-done = bf16[5120,864]{1,0:T(8,128)(2,1)} async-done(((bf16[320,864]{1,0:T(8,128)(2,1)}), bf16[5120,864]{1,0:T(8,128)(2,1)}) %all-gather.5.cloned.1.call-update) | async-done | bytes 8847376 | tf_op jit(solution)/shard_map/all_gather | solution.py:169
  270.6 12.8 %multiply_convert_fusion.1 = bf16[512,864]{0,1:T(8,128)(2,1)} fusion(f32[512,864]{0,1:T(8,128)S(1)} %fusion.51, bf16[5120,864]{1,0:T(8,128)(2,1)} %all-gather.5.cloned.1.call-done, bf16[512,5120]{1,0:T(8,128)(2,1)} %all-reduce.2.cloned.1.call-done, bf16[512,5120]{1,0:T(8,128)(2,1)} %param.26, f32[5120]{0:T(1024)S(1)} %copy-done.13, f32[512]{0:T(512)S(1)} %add_rsqrt_fusion), kind=kOutput, calls=%fused_computation.16 | convolution fusion | flops 4548231168 | bytes 22009856 | tf_op jit(solution)/shard_map/dot_general | solution.py:168
  (94 shorter events, 14.3 us)
Async XLA Ops:
  8.0 5.4 %copy-start = (bf16[512,384]{1,0:T(8,128)(2,1)S(1)}, bf16[512,384]{1,0:T(8,128)(2,1)}, u32[]{:S(2)}) copy-start(bf16[512,384]{1,0:T(8,128)(2,1)} %param.16) | copy-start | bytes 1179652
  9.3 0.5 copy-start.14
  9.8 6.2 %copy-start.9 = (f32[384]{0:T(512)S(1)}, f32[384]{0:T(512)}, u32[]{:S(2)}) copy-start(f32[384]{0:T(512)} %param.19) | copy-start | bytes 4612
  18.1 10.7 %copy-start.3 = (bf16[512,128]{1,0:T(8,128)(2,1)S(1)}, bf16[512,128]{1,0:T(8,128)(2,1)}, u32[]{:S(2)}) copy-start(bf16[512,128]{1,0:T(8,128)(2,1)} %param.17) | copy-start | bytes 393220
  18.1 12.0 %copy-start.10 = (f32[128]{0:T(128)S(1)}, f32[128]{0:T(128)}, u32[]{:S(2)}) copy-start(f32[128]{0:T(128)} %param.20) | copy-start | bytes 1540
  19.6 31.5 %all-to-all-start.2 = ((bf16[16,128,384]{2,1,0:T(8,128)(2,1)}), bf16[16,128,384]{2,1,0:T(8,128)(2,1)S(1)}, u32[]{:S(2)}, u32[]{:S(2)}) async-start(bf16[16,128,384]{2,1,0:T(8,128)(2,1)} %copy.81), calls=%async_computation.2 | async-start | bytes 3145728 | tf_op jit(solution)/shard_map/all_to_all | solution.py:134
  28.2 4.2 %copy-start.4 = (bf16[512,128]{1,0:T(8,128)(2,1)S(1)}, bf16[512,128]{1,0:T(8,128)(2,1)}, u32[]{:S(2)}) copy-start(bf16[512,128]{1,0:T(8,128)(2,1)} %param.18) | copy-start | bytes 393220
  28.7 5.0 %copy-start.7 = (s32[16,4]{0,1:T(4,128)S(1)}, s32[16,4]{0,1:T(4,128)}, u32[]{:S(2)}) copy-start(s32[16,4]{0,1:T(4,128)} %param.24) | copy-start | bytes 772
  28.8 5.0 %copy-start.8 = (s32[16,4]{0,1:T(4,128)S(1)}, s32[16,4]{0,1:T(4,128)}, u32[]{:S(2)}) copy-start(s32[16,4]{0,1:T(4,128)} %param.23) | copy-start | bytes 772
  28.8 5.0 %copy-start.11 = (f32[128]{0:T(128)S(1)}, f32[128]{0:T(128)}, u32[]{:S(2)}) copy-start(f32[128]{0:T(128)} %param.21) | copy-start | bytes 1540
  51.1 14.7 %all-to-all-start.1 = ((bf16[16,128,128]{2,1,0:T(8,128)(2,1)}), bf16[16,128,128]{2,1,0:T(8,128)(2,1)S(1)}, u32[]{:S(2)}, u32[]{:S(2)}) async-start(bf16[16,128,128]{2,1,0:T(8,128)(2,1)} %copy.77), calls=%async_computation.1 | async-start | bytes 1048576 | tf_op jit(solution)/shard_map/all_to_all | solution.py:135
  65.8 4.2 %copy-start.5 = (bf16[16,128,128]{2,1,0:T(8,128)(2,1)}, bf16[16,128,128]{2,1,0:T(8,128)(2,1)S(1)}, u32[]{:S(2)}) copy-start(bf16[16,128,128]{2,1,0:T(8,128)(2,1)S(1)} %all-to-all-done.1) | copy-start | bytes 1572868
  65.8 13.6 %all-to-all-start = ((bf16[16,128,128]{2,1,0:T(8,128)(2,1)}), bf16[16,128,128]{2,1,0:T(8,128)(2,1)}, u32[]{:S(2)}, u32[]{:S(2)}) async-start(bf16[16,128,128]{2,1,0:T(8,128)(2,1)} %copy.72), calls=%async_computation | async-start | bytes 1048576 | tf_op jit(solution)/shard_map/all_to_all | solution.py:136
  82.7 4.1 %copy-start.15 = (s32[4,1]{0,1:T(1,128)S(1)}, s32[4,1]{0,1:T(1,128)}, u32[]{:S(2)}) copy-start(s32[4,1]{0,1:T(1,128)} %copy-done.14) | copy-start | bytes 52
  82.7 4.1 %copy-start.2 = (s32[512]{0:T(512)S(1)}, s32[512]{0:T(512)}, u32[]{:S(2)}) copy-start(s32[512]{0:T(512)} %param.22) | copy-start | bytes 6148
  82.7 23.5 %all-to-all-start.3 = ((bf16[16,128,384]{1,2,0:T(8,128)(2,1)}), bf16[16,128,384]{1,2,0:T(8,128)(2,1)S(1)}, u32[]{:S(2)}, u32[]{:S(2)}) async-start(bf16[16,128,384]{1,2,0:T(8,128)(2,1)} %bitcast.106), calls=%async_computation.3 | async-start | bytes 3145728 | tf_op jit(solution)/shard_map/all_to_all | solution.py:144
  86.7 107.8 %all-reduce.2.cloned.1.call-start = ((), (), s32[]{:S(2)}) async-start(), calls=%async_computation.4 | async-start | bytes 10485760 | tf_op jit(solution)/shard_map/psum | solution.py:159
  107.1 2.0 copy-start.12
  116.0 1.3 copy-start.6
  116.0 84.4 %all-gather.3.cloned.1.call-start = ((), (), s32[]{:S(2)}) async-start(), calls=%async_computation.5 | async-start | bytes 9748480 | tf_op jit(solution)/shard_map/all_gather | solution.py:165
  116.6 154.0 %all-gather.5.cloned.1.call-start = ((), (), s32[]{:S(2)}) async-start(), calls=%async_computation.6 | async-start | bytes 9748480 | tf_op jit(solution)/shard_map/all_gather | solution.py:169
  120.0 80.4 %copy-start.13 = (f32[5120]{0:T(1024)S(1)}, f32[5120]{0:T(1024)}, u32[]{:S(2)}) copy-start(f32[5120]{0:T(1024)} %param.27) | copy-start | bytes 61444
  270.6 12.8 %copy-start.1 = (bf16[512,384]{1,0:T(8,128)(2,1)S(1)}, bf16[512,384]{1,0:T(8,128)(2,1)}, u32[]{:S(2)}) copy-start(bf16[512,384]{1,0:T(8,128)(2,1)} %param.16) | copy-start | bytes 1179652
Sparse Core Ops, SparseCore 0:
  116.1 78.3 all-reduce.1
Sparse Core Ops, SparseCore 1:
  118.6 75.8 all-gather.2
  196.5 74.0 all-gather.4
where the time goes:
time: 291 us
  waiting for transfers between devices  182 us (63%)
  matrix products  39.5 us (14%)
  starting transfers between devices  21.5 us (7%)
  local copies, waits for them, and re-layouts  20.2 us (7%)
  between operations  16 us (5%)
  other arithmetic  11.3 us (4%)
    psum x1, waiting for transfers between devices, shards(): lax.psum(jnp.dot(attn_rows, w_out, preferred_element_type=jnp.float32).as...  74.5 us
    all_gather x1, waiting for transfers between devices, shards(): lax.all_gather(w_up, 'req', axis=0, tiled=True)  58.1 us
    all_to_all x1, waiting for transfers between devices, shards(): lax.all_to_all(attended.reshape(groups_all, PAGE, q_heads * HD), 'req', s...  18.7 us
    all_to_all x1, waiting for transfers between devices, shards(): lax.all_to_all(q_send, 'req', split_axis=0, concat_axis=0, tiled=True)  16.6 us
    dot_general x1, matrix products, shards(): jnp.dot(normed, lax.all_gather(w_up, 'req', axis=0, tiled=True), preferre...  12.8 us
    dot_general x1, matrix products, shards(): jnp.dot(normed, lax.all_gather(w_gate, 'req', axis=0, tiled=True), prefer...  12.1 us
    all_to_all x1, starting transfers between devices, shards(): lax.all_to_all(q_send, 'req', split_axis=0, concat_axis=0, tiled=True)  8.6 us
    all_to_all x1, waiting for transfers between devices, shards(): lax.all_to_all(k_send, 'req', split_axis=0, concat_axis=0, tiled=True)  7.09 us
  transfers between devices with their start and end apart: 7, of which 6 were waited for; matrix products, arithmetic and copies ran while one was open for 12% of the time, Pallas kernels for 0%

commit v1 on v0

--- a/solution.py
+++ b/solution.py
@@ -156,8 +156,11 @@
         "ls,shpc->lhpc", page_select, pages_in, preferred_element_type=jnp.float32
     ).astype(jnp.bfloat16)
     attn_rows = jnp.where(alive_rows[:, None], source_rows, jnp.zeros((), jnp.bfloat16))
-    summed = lax.psum(
-        jnp.dot(attn_rows, w_out, preferred_element_type=jnp.float32).astype(jnp.bfloat16), "mp"
+    summed = jnp.sum(
+        lax.all_gather(
+            jnp.dot(attn_rows, w_out, preferred_element_type=jnp.float32).astype(jnp.bfloat16), "mp"
+        ),
+        axis=0,
     ).astype(jnp.float32)
     normed = normalize(residual, summed, norm_gain)
     gate_acc = jnp.dot(

time: 291 us -> 482 us (1.66)
  waiting for transfers between devices: 182 us -> 356 us
  other arithmetic: 11.3 us -> 29.4 us
    all_gather x0 -> x1, waiting for transfers between devices: none -> 190 us  [shards(): lax.all_gather(jnp.dot(attn_rows, w_out, preferred_element_type=jnp.float...]
    psum x1 -> x0, waiting for transfers between devices: 74.5 us -> none  [shards(): lax.psum(jnp.dot(attn_rows, w_out, preferred_element_type=jnp.float32).as...]
    all_gather x1, waiting for transfers between devices: 0.02 us -> 51.7 us  [shards(): lax.all_gather(w_gate, 'req', axis=0, tiled=True)]
    reduce_sum x0 -> x1, other arithmetic: none -> 17.9 us  [shards(): jnp.sum(lax.all_gather(jnp.dot(attn_rows, w_out, preferred_element_type=j...]
    all_gather x1, waiting for transfers between devices: 58.1 us -> 64.2 us  [shards(): lax.all_gather(w_up, 'req', axis=0, tiled=True)]
  transfers between devices with their start and end apart: 7 -> 7, of which waited for: 6 -> 7; matrix products, arithmetic and copies ran while one was open for 12% -> 11% of each run, Pallas kernels for 0% -> 0%
where the time goes in v1:
time: 482 us; the launch traced here: 481 us
  waiting for transfers between devices  356 us (74%)
  matrix products  39.6 us (8%)
  other arithmetic  29.4 us (6%)
  starting transfers between devices  21.5 us (4%)
  local copies, waits for them, and re-layouts  20.2 us (4%)
  between operations  14.2 us (3%)
    all_gather x1, waiting for transfers between devices, shards(): lax.all_gather(jnp.dot(attn_rows, w_out, preferred_element_type=jnp.float...  190 us
    all_gather x1, waiting for transfers between devices, shards(): lax.all_gather(w_up, 'req', axis=0, tiled=True)  64.2 us
    all_gather x1, waiting for transfers between devices, shards(): lax.all_gather(w_gate, 'req', axis=0, tiled=True)  51.7 us
    all_to_all x1, waiting for transfers between devices, shards(): lax.all_to_all(attended.reshape(groups_all, PAGE, q_heads * HD), 'req', s...  18.7 us
    reduce_sum x1, other arithmetic, shards(): jnp.sum(lax.all_gather(jnp.dot(attn_rows, w_out, preferred_element_type=j...  17.9 us
    all_to_all x1, waiting for transfers between devices, shards(): lax.all_to_all(q_send, 'req', split_axis=0, concat_axis=0, tiled=True)  16.6 us
    dot_general x1, matrix products, shards(): jnp.dot(normed, lax.all_gather(w_up, 'req', axis=0, tiled=True), preferre...  12.8 us
    dot_general x1, matrix products, shards(): jnp.dot(normed, lax.all_gather(w_gate, 'req', axis=0, tiled=True), prefer...  12.1 us
  transfers between devices with their start and end apart: 7, of which 7 were waited for; matrix products, arithmetic and copies ran while one was open for 11% of the time, Pallas kernels for 0%

profile of v1, /device:TPU:1, one launch (start us, length us, event | category | flops | bytes accessed | tf_op | source)
XLA Modules:
  0.0 480.9 jit_solution(12087201406264020254)
XLA Ops:
  8.9 3.6 gather_fusion
  12.6 1.9 gather_fusion.1
  17.3 1.5 copy.81
  18.8 8.6 %all-to-all-start.2 = ((bf16[16,128,384]{2,1,0:T(8,128)(2,1)}), bf16[16,128,384]{2,1,0:T(8,128)(2,1)S(1)}, u32[]{:S(2)}, u32[]{:S(2)}) async-start(bf16[16,128,384]{2,1,0:T(8,128)(2,1)} %copy.81), calls=%async_computation.2 | async-start | bytes 3145728 | tf_op jit(solution)/shard_map/all_to_all | solution.py:134
  33.7 16.6 %all-to-all-done.2 = bf16[16,128,384]{2,1,0:T(8,128)(2,1)S(1)} async-done(((bf16[16,128,384]{2,1,0:T(8,128)(2,1)}), bf16[16,128,384]{2,1,0:T(8,128)(2,1)S(1)}, u32[]{:S(2)}, u32[]{:S(2)}) %all-to-all-start.2) | async-done | bytes 1572896 | tf_op jit(solution)/shard_map/all_to_all | solution.py:134
  50.3 4.6 all-to-all-start.1
  56.2 1.7 copy.82
  57.9 7.1 %all-to-all-done.1 = bf16[16,128,128]{2,1,0:T(8,128)(2,1)S(1)} async-done(((bf16[16,128,128]{2,1,0:T(8,128)(2,1)}), bf16[16,128,128]{2,1,0:T(8,128)(2,1)S(1)}, u32[]{:S(2)}, u32[]{:S(2)}) %all-to-all-start.1) | async-done | bytes 524320 | tf_op jit(solution)/shard_map/all_to_all | solution.py:135
  65.0 4.2 all-to-all-start
  69.2 2.2 fusion
  72.4 6.2 %all-to-all-done = bf16[16,128,128]{2,1,0:T(8,128)(2,1)} async-done(((bf16[16,128,128]{2,1,0:T(8,128)(2,1)}), bf16[16,128,128]{2,1,0:T(8,128)(2,1)}, u32[]{:S(2)}, u32[]{:S(2)}) %all-to-all-start) | async-done | bytes 524320 | tf_op jit(solution)/shard_map/all_to_all | solution.py:136
  78.5 3.3 convolution_convert_fusion.1
  81.9 4.0 all-to-all-start.3
  86.7 18.7 %all-to-all-done.3 = bf16[16,128,384]{1,2,0:T(8,128)(2,1)S(1)} async-done(((bf16[16,128,384]{1,2,0:T(8,128)(2,1)}), bf16[16,128,384]{1,2,0:T(8,128)(2,1)S(1)}, u32[]{:S(2)}, u32[]{:S(2)}) %all-to-all-start.3) | async-done | bytes 1572896 | tf_op jit(solution)/shard_map/all_to_all | solution.py:144
  106.3 1.9 gather_fusion.2
  108.2 7.0 %convolution_convert_fusion = bf16[512,5120]{1,0:T(8,128)(2,1)} fusion(bf16[384,5120]{1,0:T(8,128)(2,1)} %param.25, bf16[512,384]{1,0:T(8,128)(2,1)S(1)} %gather_fusion.2, pred[512]{0:T(512)(128)(4,1)S(1)} %copy-done.12, pred[512]{0:T(512)(128)(4,1)S(1)} %broadcast_compare_fusion), kind=kOutput, calls=%fused_computation.8 | convolution fusion | flops 2016280576 | bytes 9569280 | tf_op jit(solution)/shard_map/dot_general | solution.py:161
  117.2 1.4 copy.109
  119.6 190.2 %all-gather.9.cloned.1.call-done = bf16[4096,5120]{1,0:T(8,128)(2,1)} async-done(((bf16[512,5120]{1,0:T(8,128)(2,1)}), bf16[4096,5120]{1,0:T(8,128)(2,1)}) %all-gather.9.cloned.1.call-update) | async-done | bytes 41943056 | tf_op jit(solution)/shard_map/all_gather | solution.py:160
  309.7 17.9 %reduce_sum.73 = bf16[512,5120]{1,0:T(8,128)(2,1)} reduce(bf16[8,512,5120]{2,1,0:T(8,128)(2,1)} %bitcast.104, bf16[]{:T(256)} %constant.123.clone.1), dimensions={0}, to_apply=%region_6.8 | reduce | flops 18350080 | bytes 47185920 | tf_op jit(solution)/shard_map/reduce_sum | solution.py:159
  327.7 6.0 %multiply_reduce_fusion = f32[512]{0:T(512)S(1)} fusion(bf16[512,5120]{1,0:T(8,128)(2,1)} %reduce_sum.73, bf16[512,5120]{1,0:T(8,128)(2,1)} %param.26), kind=kLoop, calls=%fused_computation.6 | loop fusion | flops 13106688 | bytes 10487808 | tf_op jit(solution)/shard_map/reduce_sum | solution.py:54
  333.7 51.7 %all-gather.5.cloned.1.call-done = bf16[5120,864]{1,0:T(8,128)(2,1)} async-done(((bf16[320,864]{1,0:T(8,128)(2,1)}), bf16[5120,864]{1,0:T(8,128)(2,1)}) %all-gather.5.cloned.1.call-update) | async-done | bytes 8847376 | tf_op jit(solution)/shard_map/all_gather | solution.py:168
  385.4 12.1 %fusion.51 = f32[512,864]{0,1:T(8,128)S(1)} fusion(bf16[5120,864]{1,0:T(8,128)(2,1)} %all-gather.5.cloned.1.call-done, bf16[512,5120]{1,0:T(8,128)(2,1)} %reduce_sum.73, bf16[512,5120]{1,0:T(8,128)(2,1)} %param.26, f32[5120]{0:T(1024)S(1)} %copy-done.13, f32[512]{0:T(512)S(1)} %add_rsqrt_fusion), kind=kOutput, calls=%fused_computation.124 | convolution fusion | flops 4545576960 | bytes 21125120 | tf_op jit(solution)/shard_map/dot_general | solution.py:166
  397.4 64.2 %all-gather.7.cloned.1.call-done = bf16[5120,864]{1,0:T(8,128)(2,1)} async-done(((bf16[320,864]{1,0:T(8,128)(2,1)}), bf16[5120,864]{1,0:T(8,128)(2,1)}) %all-gather.7.cloned.1.call-update) | async-done | bytes 8847376 | tf_op jit(solution)/shard_map/all_gather | solution.py:172
  461.6 12.8 %multiply_convert_fusion.1 = bf16[512,864]{0,1:T(8,128)(2,1)} fusion(f32[512,864]{0,1:T(8,128)S(1)} %fusion.51, bf16[5120,864]{1,0:T(8,128)(2,1)} %all-gather.7.cloned.1.call-done, bf16[512,5120]{1,0:T(8,128)(2,1)} %reduce_sum.73, bf16[512,5120]{1,0:T(8,128)(2,1)} %param.26, f32[5120]{0:T(1024)S(1)} %copy-done.13, f32[512]{0:T(512)S(1)} %add_rsqrt_fusion), kind=kOutput, calls=%fused_computation.16 | convolution fusion | flops 4548231168 | bytes 22009856 | tf_op jit(solution)/shard_map/dot_general | solution.py:171
  (95 shorter events, 17.3 us)
Async XLA Ops:
  7.2 5.4 %copy-start = (bf16[512,384]{1,0:T(8,128)(2,1)S(1)}, bf16[512,384]{1,0:T(8,128)(2,1)}, u32[]{:S(2)}) copy-start(bf16[512,384]{1,0:T(8,128)(2,1)} %param.16) | copy-start | bytes 1179652
  8.4 0.5 copy-start.14
  8.9 6.2 %copy-start.9 = (f32[384]{0:T(512)S(1)}, f32[384]{0:T(512)}, u32[]{:S(2)}) copy-start(f32[384]{0:T(512)} %param.19) | copy-start | bytes 4612
  17.2 10.7 %copy-start.3 = (bf16[512,128]{1,0:T(8,128)(2,1)S(1)}, bf16[512,128]{1,0:T(8,128)(2,1)}, u32[]{:S(2)}) copy-start(bf16[512,128]{1,0:T(8,128)(2,1)} %param.17) | copy-start | bytes 393220
  17.3 12.0 %copy-start.10 = (f32[128]{0:T(128)S(1)}, f32[128]{0:T(128)}, u32[]{:S(2)}) copy-start(f32[128]{0:T(128)} %param.20) | copy-start | bytes 1540
  18.8 31.5 %all-to-all-start.2 = ((bf16[16,128,384]{2,1,0:T(8,128)(2,1)}), bf16[16,128,384]{2,1,0:T(8,128)(2,1)S(1)}, u32[]{:S(2)}, u32[]{:S(2)}) async-start(bf16[16,128,384]{2,1,0:T(8,128)(2,1)} %copy.81), calls=%async_computation.2 | async-start | bytes 3145728 | tf_op jit(solution)/shard_map/all_to_all | solution.py:134
  27.4 4.2 copy-start.4
  27.9 5.0 %copy-start.7 = (s32[16,4]{0,1:T(4,128)S(1)}, s32[16,4]{0,1:T(4,128)}, u32[]{:S(2)}) copy-start(s32[16,4]{0,1:T(4,128)} %param.24) | copy-start | bytes 772
  27.9 5.0 %copy-start.8 = (s32[16,4]{0,1:T(4,128)S(1)}, s32[16,4]{0,1:T(4,128)}, u32[]{:S(2)}) copy-start(s32[16,4]{0,1:T(4,128)} %param.23) | copy-start | bytes 772
  27.9 5.0 %copy-start.11 = (f32[128]{0:T(128)S(1)}, f32[128]{0:T(128)}, u32[]{:S(2)}) copy-start(f32[128]{0:T(128)} %param.21) | copy-start | bytes 1540
  50.3 14.7 %all-to-all-start.1 = ((bf16[16,128,128]{2,1,0:T(8,128)(2,1)}), bf16[16,128,128]{2,1,0:T(8,128)(2,1)S(1)}, u32[]{:S(2)}, u32[]{:S(2)}) async-start(bf16[16,128,128]{2,1,0:T(8,128)(2,1)} %copy.77), calls=%async_computation.1 | async-start | bytes 1048576 | tf_op jit(solution)/shard_map/all_to_all | solution.py:135
  65.0 4.2 copy-start.5
  65.0 13.6 %all-to-all-start = ((bf16[16,128,128]{2,1,0:T(8,128)(2,1)}), bf16[16,128,128]{2,1,0:T(8,128)(2,1)}, u32[]{:S(2)}, u32[]{:S(2)}) async-start(bf16[16,128,128]{2,1,0:T(8,128)(2,1)} %copy.72), calls=%async_computation | async-start | bytes 1048576 | tf_op jit(solution)/shard_map/all_to_all | solution.py:136
  81.9 4.1 copy-start.15
  81.9 4.1 copy-start.2
  81.9 23.5 %all-to-all-start.3 = ((bf16[16,128,384]{1,2,0:T(8,128)(2,1)}), bf16[16,128,384]{1,2,0:T(8,128)(2,1)S(1)}, u32[]{:S(2)}, u32[]{:S(2)}) async-start(bf16[16,128,384]{1,2,0:T(8,128)(2,1)} %bitcast.108), calls=%async_computation.3 | async-start | bytes 3145728 | tf_op jit(solution)/shard_map/all_to_all | solution.py:144
  85.9 223.8 %all-gather.9.cloned.1.call-start = ((), (), s32[]{:S(2)}) async-start(), calls=%async_computation.6 | async-start | bytes 47185920 | tf_op jit(solution)/shard_map/all_gather | solution.py:160
  106.3 2.0 copy-start.12
  115.2 1.6 copy-start.6
  115.2 270.1 %all-gather.5.cloned.1.call-start = ((), (), s32[]{:S(2)}) async-start(), calls=%async_computation.4 | async-start | bytes 9748480 | tf_op jit(solution)/shard_map/all_gather | solution.py:168
  116.0 345.6 %all-gather.7.cloned.1.call-start = ((), (), s32[]{:S(2)}) async-start(), calls=%async_computation.5 | async-start | bytes 9748480 | tf_op jit(solution)/shard_map/all_gather | solution.py:172
  327.7 57.7 %copy-start.13 = (f32[5120]{0:T(1024)S(1)}, f32[5120]{0:T(1024)}, u32[]{:S(2)}) copy-start(f32[5120]{0:T(1024)} %param.27) | copy-start | bytes 61444
  461.6 12.8 %copy-start.1 = (bf16[512,384]{1,0:T(8,128)(2,1)S(1)}, bf16[512,384]{1,0:T(8,128)(2,1)}, u32[]{:S(2)}) copy-start(bf16[512,384]{1,0:T(8,128)(2,1)} %param.16) | copy-start | bytes 1179652
Sparse Core Ops, SparseCore 0:
  115.3 194.3 all-gather.8
  311.9 73.4 all-gather.4
  387.5 74.0 all-gather.6
